TPU v7x, 128 devices: a whole 4x4x4 slice. The times are simulated.
128 devices in a mesh: outer: 8 (over x, core), inner: 16 (over y, z).
Axes of the slice: x: 4, y: 4, z: 4, core: 2. Of those that a mesh axis runs over, the one named last changes fastest.
Arguments:
- query: bfloat16 [524288, 256], P(('outer', 'inner')), may hold values from -6 to 6
- keys: bfloat16 [524288, 256], P(('outer', 'inner')), may hold values from -1.5 to 1.5
- values: bfloat16 [524288, 256], P(('outer', 'inner')), may hold values from -6 to 6
- out_grad: bfloat16 [524288, 256], P(('outer', 'inner')), may hold values from -1.5 to 1.5
Outputs:
- attended: bfloat16 [524288, 256], P(('outer', 'inner'))
- query_grad: bfloat16 [524288, 256], P(('outer', 'inner'))
- keys_grad: bfloat16 [524288, 256], P(('outer', 'inner'))
- values_grad: bfloat16 [524288, 256], P(('outer', 'inner'))
All inputs are finite; a program needn't handle non-finite values.
Results may differ from a plain program's by a relative error of at most 0.008.
Values sent between devices are 32-bit elements; how exact they have to be, the bound alone decides.
A program may use at most 192 MiB of HBM per device.

v0:
```python
import jax
import jax.numpy as jnp
from jax import lax
from jax.sharding import PartitionSpec as P

H = 2
E = 128
BLK = 512


def prefix(part, axis, combine, identity, reverse):
    count = lax.axis_size(axis)
    place = lax.axis_index(axis)
    ahead = count - 1 - place if reverse else place
    gathered = lax.all_gather(part, axis)
    state = jnp.zeros_like(part) + jnp.asarray(identity, part.dtype)

    def one(turn, state):
        source = count - 1 - turn if reverse else turn
        return combine(state, lax.dynamic_index_in_dim(gathered, source, 0, False))

    return lax.fori_loop(0, ahead, one, state)


def add_states(earlier, later):
    return earlier + later


def state_product(form, data, state):
    high_part = state.astype(jnp.bfloat16)
    low_part = (state - high_part.astype(jnp.float32)).astype(jnp.bfloat16)
    first = jnp.einsum(form, data, high_part, preferred_element_type=jnp.float32)
    return first + jnp.einsum(form, data, low_part, preferred_element_type=jnp.float32)


def on_device(query, keys, values, out_grad):
    rows, width = query.shape
    blocks = rows // BLK
    device_index = lax.axis_index(("outer", "inner"))
    position = device_index * rows + jnp.arange(rows, dtype=jnp.int32)
    scaling = ((position.astype(jnp.float32) + 1.0) ** (-0.5)).reshape(blocks, BLK)
    query_split = query.reshape(blocks, BLK, H, E)
    keys_split = keys.reshape(blocks, BLK, H, E)
    values_split = values.reshape(blocks, BLK, H, E)
    grad_split = out_grad.reshape(blocks, BLK, H, E)
    scaled = (query_split.astype(jnp.float32) * scaling[:, :, None, None]).astype(jnp.bfloat16)
    kv_blocks = jnp.einsum(
        "nshd,nshe->nhde", keys_split, values_split, preferred_element_type=jnp.float32
    )
    qg_blocks = jnp.einsum(
        "nthd,nthe->nhde", scaled, grad_split, preferred_element_type=jnp.float32
    )
    kv_total = jnp.sum(kv_blocks, axis=0)
    qg_total = jnp.sum(qg_blocks, axis=0)
    zeros = jnp.zeros((H, E, E), jnp.float32)
    kv_before = prefix(kv_total, ("outer", "inner"), add_states, zeros, False)
    qg_after = prefix(qg_total, ("outer", "inner"), add_states, zeros, True)
    block_ids = jnp.arange(blocks, dtype=jnp.int32)
    before_mask = (block_ids[None, :] < block_ids[:, None]).astype(jnp.float32)
    after_mask = (block_ids[None, :] > block_ids[:, None]).astype(jnp.float32)
    highest = lax.Precision.HIGHEST
    kv_states = kv_before[None] + jnp.einsum(
        "mn,nhde->mhde", before_mask, kv_blocks, precision=highest
    )
    qg_states = qg_after[None] + jnp.einsum(
        "mn,nhde->mhde", after_mask, qg_blocks, precision=highest
    )
    causal = jnp.tril(jnp.ones((BLK, BLK), dtype=bool))[None, None]
    ascore = jnp.einsum("nthd,nshd->nhts", scaled, keys_split, preferred_element_type=jnp.float32)
    amat = jnp.where(causal, ascore, 0.0).astype(jnp.bfloat16)
    bscore = jnp.einsum(
        "nthe,nshe->nhts", grad_split, values_split, preferred_element_type=jnp.float32
    )
    bmat = jnp.where(causal, bscore, 0.0).astype(jnp.bfloat16)
    attended = jnp.einsum("nhts,nshe->nthe", amat, values_split, preferred_element_type=jnp.float32)
    attended = attended + state_product("nthd,nhde->nthe", scaled, kv_states)
    qgrad = jnp.einsum("nhts,nshd->nthd", bmat, keys_split, preferred_element_type=jnp.float32)
    qgrad = qgrad + state_product("nthe,nhde->nthd", grad_split, kv_states)
    qgrad = qgrad * scaling[:, :, None, None]
    kgrad = jnp.einsum("nhts,nthd->nshd", bmat, scaled, preferred_element_type=jnp.float32)
    kgrad = kgrad + state_product("nshe,nhde->nshd", values_split, qg_states)
    vgrad = jnp.einsum("nhts,nthe->nshe", amat, grad_split, preferred_element_type=jnp.float32)
    vgrad = vgrad + state_product("nshd,nhde->nshe", keys_split, qg_states)
    return (
        attended.reshape(rows, width).astype(jnp.bfloat16),
        qgrad.reshape(rows, width).astype(jnp.bfloat16),
        kgrad.reshape(rows, width).astype(jnp.bfloat16),
        vgrad.reshape(rows, width).astype(jnp.bfloat16),
    )


def solution(mesh):
    return jax.shard_map(
        on_device,
        mesh=mesh,
        in_specs=(
            P(("outer", "inner"), None),
            P(("outer", "inner"), None),
            P(("outer", "inner"), None),
            P(("outer", "inner"), None),
        ),
        out_specs=(
            P(("outer", "inner"), None),
            P(("outer", "inner"), None),
            P(("outer", "inner"), None),
            P(("outer", "inner"), None),
        ),
        check_vma=False,
    )
```

profile of v0, /device:TPU:0, one launch (start us, length us, event | category | flops | bytes accessed | tf_op | source)
XLA Modules:
  0.0 387.4 jit_solution(16393195096246319014)
XLA Ops:
  7.2 2.6 reshape.49
  9.8 4.3 %reshape.48 = bf16[8,512,2,128]{3,2,1,0:T(2,128)(2,1)} reshape(bf16[4096,256]{1,0:T(8,128)(2,1)} %param.9) | data formatting | bytes 4194304 | tf_op jit(solution)/shard_map/reshape | solution.py:43
  14.1 4.1 %fusion.40 = (f32[2,128,128]{2,1,0:T(8,128)}, f32[8,2,128,128]{3,2,1,0:T(8,128)}) fusion(bf16[8,512,2,128]{3,2,1,0:T(2,128)(2,1)S(1)} %reshape.49, bf16[8,512,2,128]{3,2,1,0:T(2,128)(2,1)} %reshape.48), kind=kOutput, calls=%fused_computation.59 | convolution fusion | flops 268664832 | bytes 5373952 | tf_op jit(solution)/shard_map/nshd,nshe->nhde/dot_general | solution.py:47
  18.3 2.6 reshape.50
  20.9 5.1 %reshape.56 = f32[8,512,2,128]{3,2,1,0:T(2,128)} reshape(bf16[4096,256]{1,0:T(8,128)(2,1)} %param.8) | data formatting | bytes 6291456 | tf_op jit(solution)/shard_map/convert_element_type | solution.py:46
  26.0 2.9 fusion.4
  30.7 8.1 %select_convert_fusion.1 = bf16[8,2,512,512]{3,2,1,0:T(8,128)(2,1)} fusion(bf16[8,512,2,128]{3,1,2,0:T(8,128)(2,1)} %copy-done, pred[512,512]{1,0:T(8,128)(4,1)S(1)} %iota_compare_fusion, bf16[8,512,2,128]{3,2,1,0:T(2,128)(2,1)} %reshape.48), kind=kOutput, calls=%fused_computation.3 | convolution fusion | flops 1082130432 | bytes 12845056 | tf_op jit(solution)/shard_map/nthd,nshd->nhts/dot_general | solution.py:69
  38.8 2.5 select_convert_fusion
  41.3 3.2 copy-done.7
  44.5 3.5 fusion.42
  48.0 52.8 %all-gather.5.cloned.1.call-done = f32[256,128,128]{2,1,0:T(8,128)} async-done(((f32[2,128,128]{2,1,0:T(8,128)}), f32[256,128,128]{2,1,0:T(8,128)}) %all-gather.5.cloned.1.call-update) | async-done | bytes 16777232 | tf_op jit(solution)/shard_map/all_gather | solution.py:15
  101.1 2.5 subtract_convert_fusion.1
  103.6 2.7 fusion.11
  106.3 2.6 fusion.33
  109.0 2.7 fusion.9
  111.6 2.7 fusion.30
  114.3 69.2 %all-gather.7.cloned.1.call-done = f32[256,128,128]{2,1,0:T(8,128)} async-done(((f32[2,128,128]{2,1,0:T(8,128)}), f32[256,128,128]{2,1,0:T(8,128)}) %all-gather.7.cloned.1.call-update) | async-done | bytes 16777232 | tf_op jit(solution)/shard_map/all_gather | solution.py:15
  183.5 121.9 %while.23 = (s32[]{:T(128)}, f32[2,128,128]{2,1,0:T(8,128)S(1)}, s32[]{:T(128)}, f32[128,2,128,128]{3,2,1,0:T(8,128)}, s32[]{:T(128)}, /*index=5*/s32[]{:T(128)}, s32[]{:T(128)}, s32[]{:T(128)}) while((s32[]{:T(128)}, f32[2,128,128]{2,1,0:T(8,128)S(1)}, s32[]{:T(128)}, f32[128,2,128,128]{3,2,1,0:T(8,128)}, s32[]{:T(128)}, ...), condition=%wide.region_5.6_spmd, body=%wide.region_4.5_spmd.sunk | while | flops 32774 | bytes 393359 | solution.py:22
  305.4 2.3 subtract_convert_fusion
  309.1 4.5 %fusion.24 = f32[8,2,128,512]{2,3,1,0:T(8,128)} fusion(bf16[8,2,128,128]{2,3,1,0:T(8,128)(2,1)S(1)} %copy.119, bf16[8,512,2,128]{3,2,1,0:T(2,128)(2,1)} %reshape.48), kind=kOutput, calls=%fused_computation.39 | convolution fusion | flops 268435456 | bytes 6815744 | tf_op jit(solution)/shard_map/nshd,nhde->nshe/dot_general | solution.py:32
  313.6 2.9 fusion.15
  316.5 10.1 %fusion.2 = bf16[8,512,2,128]{3,1,2,0:T(8,128)(2,1)} fusion(f32[8,2,128,512]{2,3,1,0:T(8,128)} %fusion.11, f32[8,2,128,512]{2,3,1,0:T(8,128)} %fusion.9, bf16[8,2,512,512]{3,2,1,0:T(8,128)(2,1)} %copy-done.7, f32[8,512]{1,0:T(8,128)S(1)} %add_power_fusion, bf16[8,512,2,128]{3,2,1,0:T(2,128)(2,1)S(1)} %copy-done.8), kind=kOutput, calls=%fused_computation.8 | convolution fusion | flops 1077936128 | bytes 20987904 | tf_op jit(solution)/shard_map/nhts,nshd->nthd/dot_general | solution.py:77
  326.6 5.1 %copy.144 = bf16[8,512,2,128]{3,2,1,0:T(2,128)(2,1)} copy(bf16[8,512,2,128]{3,1,2,0:T(8,128)(2,1)} %fusion.2) | data formatting | bytes 4194304
  331.7 6.1 %fusion.3 = bf16[8,512,2,128]{3,1,2,0:T(8,128)(2,1)S(1)} fusion(f32[8,2,128,512]{2,3,1,0:T(8,128)} %fusion.33, f32[8,2,128,512]{2,3,1,0:T(8,128)} %fusion.30, bf16[8,2,512,512]{3,2,1,0:T(8,128)(2,1)S(1)} %bitcast.76, bf16[8,512,2,128]{3,2,1,0:T(2,128)(2,1)S(1)} %copy-done.5), kind=kOutput, calls=%fused_computation.10 | convolution fusion | flops 1076887552 | bytes 20971520 | tf_op jit(solution)/shard_map/nhts,nshe->nthe/dot_general | solution.py:75
  337.8 3.7 copy.143
  341.9 4.2 %fusion.22 = f32[8,2,128,512]{2,3,1,0:T(8,128)} fusion(bf16[8,2,128,128]{2,3,1,0:T(8,128)(2,1)S(1)} %copy.121, bf16[8,512,2,128]{3,2,1,0:T(2,128)(2,1)} %reshape.48), kind=kOutput, calls=%fused_computation.37 | convolution fusion | flops 268435456 | bytes 6815744 | tf_op jit(solution)/shard_map/nshd,nhde->nshe/dot_general | solution.py:33
  346.1 10.0 %fusion = bf16[8,512,2,128]{3,1,2,0:T(8,128)(2,1)} fusion(f32[8,2,128,512]{2,3,1,0:T(8,128)} %fusion.24, f32[8,2,128,512]{2,3,1,0:T(8,128)} %fusion.22, bf16[8,2,512,512]{3,2,1,0:T(8,128)(2,1)} %select_convert_fusion.1, bf16[8,512,2,128]{3,2,1,0:T(2,128)(2,1)S(1)} %reshape.50), kind=kOutput, calls=%fused_computation.5 | convolution fusion | flops 1076887552 | bytes 20971520 | tf_op jit(solution)/shard_map/nhts,nthe->nshe/dot_general | solution.py:82
  356.1 5.2 %copy.146 = bf16[8,512,2,128]{3,2,1,0:T(2,128)(2,1)} copy(bf16[8,512,2,128]{3,1,2,0:T(8,128)(2,1)} %fusion) | data formatting | bytes 4194304
  361.3 5.7 %fusion.5 = bf16[8,512,2,128]{1,3,2,0:T(8,128)(2,1)} fusion(f32[8,2,128,512]{3,2,1,0:T(8,128)} %fusion.42, f32[8,2,128,512]{3,2,1,0:T(8,128)} %fusion.15, bf16[8,2,128,128]{2,3,1,0:T(8,128)(2,1)S(1)} %copy.121, bf16[8,512,2,128]{3,2,1,0:T(2,128)(2,1)S(1)} %copy-done.6), kind=kOutput, calls=%fused_computation.18 | convolution fusion | flops 271581184 | bytes 13107200 | tf_op jit(solution)/shard_map/nshe,nhde->nshd/dot_general | solution.py:33
  367.0 6.3 %copy.145 = bf16[8,512,2,128]{3,2,1,0:T(2,128)(2,1)} copy(bf16[8,512,2,128]{1,3,2,0:T(8,128)(2,1)} %fusion.5) | data formatting | bytes 4194304
  373.3 4.4 %copy_bitcast_fusion.2 = (bf16[4096,256]{1,0:T(8,128)(2,1)}, bf16[4096,256]{1,0:T(8,128)(2,1)}) fusion(bf16[512,8,2,128]{3,2,1,0:T(2,128)(2,1)S(1)} %bitcast.77, bf16[512,8,2,128]{3,2,1,0:T(2,128)(2,1)} %bitcast.78), kind=kLoop, calls=%fused_computation.16 | loop fusion | bytes 8388608
  377.7 2.9 copy_bitcast_fusion
  (169 shorter events, 122.8 us)
Async XLA Ops:
  7.2 93.7 %all-gather.5.cloned.1.call-start = ((), (), s32[]{:S(2)}) async-start(), calls=%async_computation | async-start | bytes 16908288 | tf_op jit(solution)/shard_map/all_gather | solution.py:15
  9.8 4.4 %copy-start.3 = (bf16[8,512,2,128]{3,2,1,0:T(2,128)(2,1)}, bf16[8,512,2,128]{3,2,1,0:T(2,128)(2,1)S(1)}, u32[]{:S(2)}) copy-start(bf16[8,512,2,128]{3,2,1,0:T(2,128)(2,1)S(1)} %reshape.49) | copy-start | bytes 6291460
  18.3 165.2 %all-gather.7.cloned.1.call-start = ((), (), s32[]{:S(2)}) async-start(), calls=%async_computation.1 | async-start | bytes 16908288 | tf_op jit(solution)/shard_map/all_gather | solution.py:15
  28.9 1.6 copy-start
  30.7 8.1 %copy-start.4 = (bf16[8,512,2,128]{3,2,1,0:T(2,128)(2,1)S(1)}, bf16[8,512,2,128]{3,2,1,0:T(2,128)(2,1)}, u32[]{:S(2)}) copy-start(bf16[8,512,2,128]{3,2,1,0:T(2,128)(2,1)} %copy-done.3) | copy-start | bytes 6291460
  38.8 5.7 %copy-start.1 = (bf16[8,512,2,128]{3,1,2,0:T(8,128)(2,1)S(1)}, bf16[8,512,2,128]{3,1,2,0:T(8,128)(2,1)}, u32[]{:S(2)}) copy-start(bf16[8,512,2,128]{3,1,2,0:T(8,128)(2,1)} %copy-done) | copy-start | bytes 6291460
  41.3 3.2 copy-start.7
  103.6 2.7 copy-start.2
  309.1 4.5 %copy-start.5 = (bf16[8,512,2,128]{3,2,1,0:T(2,128)(2,1)S(1)}, bf16[8,512,2,128]{3,2,1,0:T(2,128)(2,1)}, u32[]{:S(2)}) copy-start(bf16[8,512,2,128]{3,2,1,0:T(2,128)(2,1)} %copy-done.3) | copy-start | bytes 6291460
  313.6 2.9 copy-start.8
  313.6 18.1 %slice-start = ((s8[8388608]{0:T(1024)(128)(4,1)}), s8[4194304]{0:T(1024)(128)(4,1)S(1)}, s32[]{:S(2)}) async-start(s8[8388608]{0:T(1024)(128)(4,1)} %bitcast.75), calls=%async_computation.2 | async-start | bytes 8388608
  316.5 15.2 %slice-start.1 = ((s8[8388608]{0:T(1024)(128)(4,1)}), s8[4194304]{0:T(1024)(128)(4,1)S(1)}, s32[]{:S(2)}) async-start(s8[8388608]{0:T(1024)(128)(4,1)} %bitcast.75), calls=%async_computation.3 | async-start | bytes 8388608
  337.7 3.7 copy-start.12
  356.1 5.2 %copy-start.6 = (bf16[8,512,2,128]{3,2,1,0:T(2,128)(2,1)S(1)}, bf16[8,512,2,128]{3,2,1,0:T(2,128)(2,1)}, u32[]{:S(2)}) copy-start(bf16[8,512,2,128]{3,2,1,0:T(2,128)(2,1)} %copy-done.3) | copy-start | bytes 6291460
  366.9 6.3 %copy-start.9 = (bf16[8,512,2,128]{3,2,1,0:T(2,128)(2,1)S(1)}, bf16[8,512,2,128]{3,2,1,0:T(2,128)(2,1)}, u32[]{:S(2)}) copy-start(bf16[8,512,2,128]{3,2,1,0:T(2,128)(2,1)} %copy.144) | copy-start | bytes 6291460
  373.3 4.4 %copy-start.10 = (bf16[8,512,2,128]{3,2,1,0:T(2,128)(2,1)S(1)}, bf16[8,512,2,128]{3,2,1,0:T(2,128)(2,1)}, u32[]{:S(2)}) copy-start(bf16[8,512,2,128]{3,2,1,0:T(2,128)(2,1)} %copy.146) | copy-start | bytes 6291460
  373.3 4.4 %copy-start.11 = (bf16[8,512,2,128]{3,2,1,0:T(2,128)(2,1)S(1)}, bf16[8,512,2,128]{3,2,1,0:T(2,128)(2,1)}, u32[]{:S(2)}) copy-start(bf16[8,512,2,128]{3,2,1,0:T(2,128)(2,1)} %copy.145) | copy-start | bytes 6291460
Sparse Core Ops, SparseCore 0:
  18.4 82.4 all-gather.4
  104.0 79.4 all-gather.6
where the time goes:
time: 390 us; the launch traced here: 387 us
  waiting for transfers between devices  122 us (31%)
  other arithmetic  122 us (31%)
  matrix products  78.7 us (20%)
  local copies, waits for them, and re-layouts  47.2 us (12%)
  between operations  14.2 us (4%)
    all_gather x2, waiting for transfers between devices, prefix(): gathered = lax.all_gather(part, axis)  122 us
    add x127, other arithmetic, add_states(): return earlier + later  119 us
    unnamed x36, local copies, waits for them, and re-layouts  30.9 us
    dot_general x4, matrix products, state_product(): jnp.einsum(form, data, low_part, preferred_element_type=jnp.float32)  15.2 us
    dot_general x4, matrix products, state_product(): jnp.einsum(form, data, high_part, preferred_element_type=jnp.float32)  12.7 us
    dot_general x1, matrix products, on_device(): jnp.einsum('nhts,nshd->nthd', bmat, keys_split, preferred_element_type=jn...  10.1 us
    dot_general x1, matrix products, on_device(): jnp.einsum('nhts,nthe->nshe', amat, grad_split, preferred_element_type=jn...  9.96 us
    dot_general x1, matrix products, on_device(): jnp.einsum('nthd,nshd->nhts', scaled, keys_split, preferred_element_type=...  8.12 us
  transfers between devices with their start and end apart: 2, of which 2 were waited for; matrix products, arithmetic and copies ran while one was open for 10% of the time, Pallas kernels for 0%

commit v1 on v0

v1 whole, which is shorter than its diff:
```python
import functools

import jax
import jax.numpy as jnp
from jax import lax
from jax.experimental import pallas as pl
from jax.experimental.pallas import tpu as pltpu
from jax.sharding import PartitionSpec as P

H = 2
E = 128
TILE = 256
CHUNK = 512
STEP = 1024
MESH = pl.DeviceIdType.MESH
F32 = jnp.float32
BF16 = jnp.bfloat16
NN = (((1,), (0,)), ((), ()))
NT = (((1,), (1,)), ((), ()))
TN = (((0,), (0,)), ((), ()))


def dot(a, b, dims):
    return lax.dot_general(a, b, dims, preferred_element_type=F32)


def coefficient(first, rows):
    place = lax.broadcasted_iota(jnp.int32, (rows, E), 0) + first
    return lax.rsqrt(place.astype(F32) + 1.0)


def states_kernel(
    n_outer, n_inner,
    query, keys, values, grad,
    kv_states, qg_states,
    q_in, k_in, v_in, g_in, kv_local, qg_local,
    mine, arrived, done, total, totals, finished,
    in_sem, send_a, recv_a, send_b, recv_b, send_c, recv_c,
):
    outer = lax.axis_index("outer")
    inner = lax.axis_index("inner")
    rows = query.shape[0]
    chunks = rows // CHUNK
    per_chunk = CHUNK // TILE
    part = E * H // n_inner

    def load(which, source, target, chunk):
        span = pl.ds(pl.multiple_of(chunk * CHUNK, CHUNK), CHUNK)
        return pltpu.make_async_copy(source.at[span], target.at[span], in_sem.at[which, chunk])

    @pl.loop(0, chunks)
    def _(chunk):
        load(0, keys, k_in, chunk).start()
        load(1, values, v_in, chunk).start()
        load(2, query, q_in, chunks - 1 - chunk).start()
        load(3, grad, g_in, chunks - 1 - chunk).start()

    barrier = pltpu.get_barrier_semaphore()

    @pl.loop(1, n_inner)
    def _(step):
        peer = lax.rem(inner + step, n_inner)
        pl.semaphore_signal(barrier, inc=1, device_id=(outer, peer), device_id_type=MESH)

    @pl.loop(1, n_outer)
    def _(step):
        peer = lax.rem(outer + step, n_outer)
        pl.semaphore_signal(barrier, inc=1, device_id=(peer, inner), device_id_type=MESH)

    first = (outer * n_inner + inner) * rows

    def accumulate(chunk, sums):
        kv, qg = list(sums[:H]), list(sums[H:])
        load(0, keys, k_in, chunk).wait()
        load(1, values, v_in, chunk).wait()
        for b in range(per_chunk):
            block = chunk * per_chunk + b
            span = pl.ds(pl.multiple_of(block * TILE, TILE), TILE)
            for h in range(H):
                cols = slice(h * E, (h + 1) * E)
                kv_local[block, h] = kv[h]
                kv[h] = kv[h] + dot(k_in[span, cols], v_in[span, cols], TN)
        back = chunks - 1 - chunk
        load(2, query, q_in, back).wait()
        load(3, grad, g_in, back).wait()
        for b in range(per_chunk - 1, -1, -1):
            block = back * per_chunk + b
            span = pl.ds(pl.multiple_of(block * TILE, TILE), TILE)
            scale = coefficient(first + block * TILE, TILE)
            for h in range(H):
                cols = slice(h * E, (h + 1) * E)
                qg_local[block, h] = qg[h]
                scaled = (q_in[span, cols].astype(F32) * scale).astype(BF16)
                qg[h] = qg[h] + dot(scaled, g_in[span, cols], TN)
        return tuple(kv) + tuple(qg)

    zero = jnp.zeros((E, E), F32)
    sums = lax.fori_loop(0, chunks, accumulate, (zero,) * (2 * H))
    for h in range(H):
        share = n_inner // H
        mine[h * share:(h + 1) * share, 0:part] = sums[h].reshape(share, part, E)
        mine[h * share:(h + 1) * share, part:2 * part] = sums[H + h].reshape(share, part, E)

    pl.semaphore_wait(barrier, n_inner + n_outer - 2)

    def hand_out(step):
        peer = lax.rem(inner + step, n_inner)
        return pltpu.make_async_remote_copy(
            src_ref=mine.at[peer], dst_ref=arrived.at[inner],
            send_sem=send_a.at[peer], recv_sem=recv_a.at[inner],
            device_id=(outer, peer), device_id_type=MESH)

    def take_in(step):
        peer = lax.rem(inner + step, n_inner)
        return pltpu.make_async_remote_copy(
            src_ref=mine.at[peer], dst_ref=arrived.at[peer],
            send_sem=send_a.at[peer], recv_sem=recv_a.at[peer],
            device_id=(outer, peer), device_id_type=MESH)

    @pl.loop(1, n_inner)
    def _(step):
        hand_out(step).start()

    arrived[inner] = mine[inner]

    @pl.loop(1, n_inner)
    def _(step):
        take_in(step).wait_recv()

    kv = jnp.zeros((part, E), F32)
    qg = jnp.zeros((part, E), F32)
    for j in range(n_inner):
        done[j, 0:part] = kv
        kv = kv + arrived[j, 0:part]
        k = n_inner - 1 - j
        done[k, part:2 * part] = qg
        qg = qg + arrived[k, part:2 * part]
    total[0:part] = kv
    total[part:2 * part] = qg

    def spread(step):
        peer = lax.rem(outer + step, n_outer)
        return pltpu.make_async_remote_copy(
            src_ref=total, dst_ref=totals.at[outer],
            send_sem=send_b.at[peer], recv_sem=recv_b.at[outer],
            device_id=(peer, inner), device_id_type=MESH)

    def collect(step):
        peer = lax.rem(outer + step, n_outer)
        return pltpu.make_async_remote_copy(
            src_ref=total, dst_ref=totals.at[peer],
            send_sem=send_b.at[peer], recv_sem=recv_b.at[peer],
            device_id=(peer, inner), device_id_type=MESH)

    @pl.loop(1, n_outer)
    def _(step):
        spread(step).start()

    totals[outer] = total[...]

    @pl.loop(1, n_outer)
    def _(step):
        collect(step).wait_recv()

    kv = jnp.zeros((part, E), F32)
    qg = jnp.zeros((part, E), F32)
    for j in range(n_outer):
        kv = kv + jnp.where(j < outer, totals[j, 0:part], 0.0)
        qg = qg + jnp.where(j > outer, totals[j, part:2 * part], 0.0)
    for j in range(n_inner):
        done[j, 0:part] = done[j, 0:part] + kv
        done[j, part:2 * part] = done[j, part:2 * part] + qg

    def hand_back(step):
        peer = lax.rem(inner + step, n_inner)
        return pltpu.make_async_remote_copy(
            src_ref=done.at[peer], dst_ref=finished.at[inner],
            send_sem=send_c.at[peer], recv_sem=recv_c.at[inner],
            device_id=(outer, peer), device_id_type=MESH)

    def take_back(step):
        peer = lax.rem(inner + step, n_inner)
        return pltpu.make_async_remote_copy(
            src_ref=done.at[peer], dst_ref=finished.at[peer],
            send_sem=send_c.at[peer], recv_sem=recv_c.at[peer],
            device_id=(outer, peer), device_id_type=MESH)

    @pl.loop(1, n_inner)
    def _(step):
        hand_back(step).start()

    finished[inner] = done[inner]

    @pl.loop(1, n_inner)
    def _(step):
        take_back(step).wait_recv()

    share = n_inner // H
    for h in range(H):
        span = slice(h * share, (h + 1) * share)
        kv = finished[span, 0:part].reshape(E, E)
        qg = finished[span, part:2 * part].reshape(E, E)

        @pl.loop(0, rows // TILE)
        def _(block):
            kv_states[block, h] = (kv_local[block, h] + kv).astype(BF16)
            qg_states[block, h] = (qg_local[block, h] + qg).astype(BF16)

    @pl.loop(1, n_inner)
    def _(step):
        hand_out(step).wait_send()
        hand_back(step).wait_send()

    @pl.loop(1, n_outer)
    def _(step):
        spread(step).wait_send()


def outputs_kernel(n_inner, total_rows, query, keys, values, grad, kv_states, qg_states, attended, qgrad, kgrad, vgrad):
    outer = lax.axis_index("outer")
    inner = lax.axis_index("inner")
    first = (outer * n_inner + inner) * total_rows + pl.program_id(0) * STEP
    row = lax.broadcasted_iota(jnp.int32, (TILE, TILE), 0)
    col = lax.broadcasted_iota(jnp.int32, (TILE, TILE), 1)
    causal = row >= col
    zero = jnp.zeros((E, E), BF16)

    def both(state):
        top = jnp.concatenate([state[0], zero], axis=1)
        bottom = jnp.concatenate([zero, state[1]], axis=1)
        return jnp.concatenate([top, bottom], axis=0)

    for b in range(STEP // TILE):
        span = slice(b * TILE, (b + 1) * TILE)
        scale = coefficient(first + b * TILE, TILE)
        wide = jnp.concatenate([scale] * H, axis=1)
        scaled = (query[span].astype(F32) * wide).astype(BF16)
        k, v, g = keys[span], values[span], grad[span]
        kv, qg = both(kv_states[b]), both(qg_states[b])
        state_parts = (dot(scaled, kv, NN), dot(g, kv, NT), dot(v, qg, NT), dot(k, qg, NN))
        for h in range(H):
            cols = slice(h * E, (h + 1) * E)
            a = jnp.where(causal, dot(scaled[:, cols], k[:, cols], NT), 0.0).astype(BF16)
            d = jnp.where(causal, dot(g[:, cols], v[:, cols], NT), 0.0).astype(BF16)
            attended[span, cols] = (dot(a, v[:, cols], NN) + state_parts[0][:, cols]).astype(BF16)
            qgrad[span, cols] = ((dot(d, k[:, cols], NN) + state_parts[1][:, cols]) * scale).astype(BF16)
            kgrad[span, cols] = (dot(d, scaled[:, cols], TN) + state_parts[2][:, cols]).astype(BF16)
            vgrad[span, cols] = (dot(a, g[:, cols], TN) + state_parts[3][:, cols]).astype(BF16)


def on_device(n_outer, n_inner, query, keys, values, out_grad):
    rows, width = query.shape
    blocks = rows // TILE
    part = E * H // n_inner
    anywhere = pl.BlockSpec(memory_space=pl.ANY)
    in_vmem = pl.BlockSpec(memory_space=pltpu.VMEM)
    slices = pltpu.VMEM((n_inner, 2 * part, E), F32)
    dma = pltpu.SemaphoreType.DMA
    states = jax.ShapeDtypeStruct((blocks, H, E, E), BF16)
    kv_states, qg_states = pl.pallas_call(
        functools.partial(states_kernel, n_outer, n_inner),
        out_shape=(states, states),
        in_specs=[anywhere] * 4,
        out_specs=(in_vmem, in_vmem),
        scratch_shapes=[pltpu.VMEM((rows, width), BF16)] * 4
        + [pltpu.VMEM((blocks, H, E, E), F32)] * 2
        + [slices, slices, slices, pltpu.VMEM((2 * part, E), F32),
           pltpu.VMEM((n_outer, 2 * part, E), F32), slices]
        + [dma((4, rows // CHUNK)), dma((n_inner,)), dma((n_inner,)), dma((n_outer,)),
           dma((n_outer,)), dma((n_inner,)), dma((n_inner,))],
        compiler_params=pltpu.CompilerParams(
            collective_id=0, has_side_effects=True, vmem_limit_bytes=32 << 20),
        name="states",
    )(query, keys, values, out_grad)
    data = pl.BlockSpec((STEP, width), lambda i: (i, 0))
    state = pl.BlockSpec((STEP // TILE, H, E, E), lambda i: (i, 0, 0, 0))
    result = jax.ShapeDtypeStruct((rows, width), BF16)
    return pl.pallas_call(
        functools.partial(outputs_kernel, n_inner, rows),
        grid=(rows // STEP,),
        out_shape=(result,) * 4,
        in_specs=[data] * 4 + [state] * 2,
        out_specs=(data,) * 4,
        compiler_params=pltpu.CompilerParams(vmem_limit_bytes=32 << 20),
        name="outputs",
    )(query, keys, values, out_grad, kv_states, qg_states)


def solution(mesh):
    spec = P(("outer", "inner"), None)
    return jax.shard_map(
        functools.partial(on_device, mesh.shape["outer"], mesh.shape["inner"]),
        mesh=mesh,
        in_specs=(spec,) * 4,
        out_specs=(spec,) * 4,
        check_vma=False,
    )
```

time: 390 us -> 50.7 us (0.13)
  other arithmetic: 122 us -> 0 us
  waiting for transfers between devices: 122 us -> 0 us
  matrix products: 78.7 us -> 0 us
  Pallas kernels: 0 us -> 43.5 us
  local copies, waits for them, and re-layouts: 47.2 us -> 6.36 us
  between operations: 14.2 us -> 0.65 us
    all_gather x2 -> x0, waiting for transfers between devices: 122 us -> none  [prefix(): gathered = lax.all_gather(part, axis)]
    add x127 -> x0, other arithmetic: 119 us -> none  [add_states(): return earlier + later]
    dot_general x18 -> x0, matrix products: 78.7 us -> none  [the longest x4 15.2 us: state_product(): jnp.einsum(form, data, low_part, preferred_element_type=jnp.float32)]
    pallas_call x0 -> x2, Pallas kernels: none -> 43.5 us  [the longest x1 28.1 us: on_device(): pl.pallas_call(functools.partial(states_kernel, n_outer, n_inner), out_sh...]
    unnamed x36 -> x8, local copies, waits for them, and re-layouts: 30.9 us -> 6.36 us
    reshape x3 -> x0, local copies, waits for them, and re-layouts: 9.44 us -> none  [the longest x1 4.34 us: on_device(): keys_split = keys.reshape(blocks, BLK, H, E)]
    convert_element_type x3 -> x0, local copies, waits for them, and re-layouts: 6.87 us -> none  [the longest x1 5.11 us: on_device(): query_split.astype(jnp.float32) * scaling[:, :, None, None]]
  transfers between devices with their start and end apart: 2 -> 0, of which waited for: 2 -> 0; matrix products, arithmetic and copies ran while one was open for 10% -> 0% of each run, Pallas kernels for 0% -> 0%
where the time goes in v1:
time: 50.7 us; the launch traced here: 50.5 us
  Pallas kernels  43.5 us (86%)
  local copies, waits for them, and re-layouts  6.36 us (13%)
  between operations  0.65 us (1%)
    pallas_call x1, Pallas kernels, on_device(): pl.pallas_call(functools.partial(states_kernel, n_outer, n_inner), out_sh...  28.1 us
    pallas_call x1, Pallas kernels, on_device(): pl.pallas_call(functools.partial(outputs_kernel, n_inner, rows), grid=(ro...  15.4 us
    unnamed x8, local copies, waits for them, and re-layouts  6.36 us

profile of v1, /device:TPU:0, one launch (start us, length us, event | category | flops | bytes accessed | tf_op | source)
XLA Modules:
  0.0 50.5 jit_solution(8747956902522813094)
XLA Ops:
  0.6 0.0 copy-start
  0.6 1.6 %copy-done = bf16[4096,256]{1,0:T(8,128)(2,1)S(1)} copy-done((bf16[4096,256]{1,0:T(8,128)(2,1)S(1)}, bf16[4096,256]{1,0:T(8,128)(2,1)}, u32[]{:S(2)}) %copy-start) | copy-done | bytes 2097176
  2.2 0.0 copy-start.1
  2.2 1.6 %copy-done.1 = bf16[4096,256]{1,0:T(8,128)(2,1)S(1)} copy-done((bf16[4096,256]{1,0:T(8,128)(2,1)S(1)}, bf16[4096,256]{1,0:T(8,128)(2,1)}, u32[]{:S(2)}) %copy-start.1) | copy-done | bytes 2097176
  3.8 0.0 copy-start.2
  3.8 1.6 %copy-done.2 = bf16[4096,256]{1,0:T(8,128)(2,1)S(1)} copy-done((bf16[4096,256]{1,0:T(8,128)(2,1)S(1)}, bf16[4096,256]{1,0:T(8,128)(2,1)}, u32[]{:S(2)}) %copy-start.2) | copy-done | bytes 2097176
  5.4 0.0 copy-start.3
  5.4 1.6 %copy-done.3 = bf16[4096,256]{1,0:T(8,128)(2,1)S(1)} copy-done((bf16[4096,256]{1,0:T(8,128)(2,1)S(1)}, bf16[4096,256]{1,0:T(8,128)(2,1)}, u32[]{:S(2)}) %copy-start.3) | copy-done | bytes 2097176
  7.0 28.1 %states.1 = (bf16[16,2,128,128]{3,2,1,0:T(8,128)(2,1)S(1)}, bf16[16,2,128,128]{3,2,1,0:T(8,128)(2,1)S(1)}) custom-call(bf16[4096,256]{1,0:T(8,128)(2,1)S(1)} %copy-done, bf16[4096,256]{1,0:T(8,128)(2,1)S(1)} %copy-done.1, bf16[4096,256]{1,0:T(8,128)(2,1)S(1)} %copy-done.2, bf16[4096,256]{1,0:T(8,128)(2,1)S(1)} %copy-done.3), custom_call_target="tpu_custom_call" | custom-call | tf_op jit(solution)/shard_map/states/pallas_call | solution.py:260
  35.1 15.4 %outputs.1 = (bf16[4096,256]{1,0:T(8,128)(2,1)}, bf16[4096,256]{1,0:T(8,128)(2,1)}, bf16[4096,256]{1,0:T(8,128)(2,1)}, bf16[4096,256]{1,0:T(8,128)(2,1)}) custom-call(bf16[4096,256]{1,0:T(8,128)(2,1)S(1)} %copy-done, bf16[4096,256]{1,0:T(8,128)(2,1)S(1)} %copy-done.1, bf16[4096,256]{1,0:T(8,128)(2,1)S(1)} %copy-done.2, bf16[4096,256]{1,0:T(8,128)(2,1)S(1)} %copy-done.3, ...), custom_call_target="tpu_custom_call" | custom-call | tf_op jit(solution)/shard_map/outputs/pallas_call | solution.py:278
Async XLA Ops:
  0.6 1.6 %copy-start = (bf16[4096,256]{1,0:T(8,128)(2,1)S(1)}, bf16[4096,256]{1,0:T(8,128)(2,1)}, u32[]{:S(2)}) copy-start(bf16[4096,256]{1,0:T(8,128)(2,1)} %query.3) | copy-start | bytes 6291460
  2.2 1.6 %copy-start.1 = (bf16[4096,256]{1,0:T(8,128)(2,1)S(1)}, bf16[4096,256]{1,0:T(8,128)(2,1)}, u32[]{:S(2)}) copy-start(bf16[4096,256]{1,0:T(8,128)(2,1)} %keys.3) | copy-start | bytes 6291460
  3.8 1.6 %copy-start.2 = (bf16[4096,256]{1,0:T(8,128)(2,1)S(1)}, bf16[4096,256]{1,0:T(8,128)(2,1)}, u32[]{:S(2)}) copy-start(bf16[4096,256]{1,0:T(8,128)(2,1)} %values.3) | copy-start | bytes 6291460
  5.4 1.6 %copy-start.3 = (bf16[4096,256]{1,0:T(8,128)(2,1)S(1)}, bf16[4096,256]{1,0:T(8,128)(2,1)}, u32[]{:S(2)}) copy-start(bf16[4096,256]{1,0:T(8,128)(2,1)} %grad.3) | copy-start | bytes 6291460

commit v2 on v1

v2 whole, which is shorter than its diff:
```python
import functools

import jax
import jax.numpy as jnp
from jax import lax
from jax.experimental import pallas as pl
from jax.experimental.pallas import tpu as pltpu
from jax.sharding import PartitionSpec as P

H = 2
E = 128
TILE = 256
CHUNK = 512
OUT = 512
SPLIT = (3, 6, 8)
MESH = pl.DeviceIdType.MESH
F32 = jnp.float32
BF16 = jnp.bfloat16
NN = (((1,), (0,)), ((), ()))
NT = (((1,), (1,)), ((), ()))
TN = (((0,), (0,)), ((), ()))


def dot(a, b, dims):
    return lax.dot_general(a, b, dims, preferred_element_type=F32)


def coefficient(first, rows):
    place = lax.broadcasted_iota(jnp.int32, (rows, E), 0) + first
    return lax.rsqrt(place.astype(F32) + 1.0)


def both_heads(first, second):
    zero = jnp.zeros((E, E), BF16)
    top = jnp.concatenate([first, zero], axis=1)
    bottom = jnp.concatenate([zero, second], axis=1)
    return jnp.concatenate([top, bottom], axis=0)


def local_kernel(
    n_outer, n_inner,
    query, keys, values, grad,
    scaled, k_in, v_in, g_in, att_sum, qgrad_sum, kgrad_sum, vgrad_sum, before,
    kv_local, qg_local, mine, arrived, done, total, totals, finished,
    in_sem, send_a, recv_a, send_b, recv_b, send_c, recv_c,
):
    outer = lax.axis_index("outer")
    inner = lax.axis_index("inner")
    rows = query.shape[0]
    chunks = rows // CHUNK
    per_chunk = CHUNK // TILE
    part = E * H // n_inner

    def load(which, source, target, chunk):
        span = pl.ds(pl.multiple_of(chunk * CHUNK, CHUNK), CHUNK)
        return pltpu.make_async_copy(source.at[span], target.at[span], in_sem.at[which, chunk])

    @pl.loop(0, chunks)
    def _(chunk):
        load(0, keys, k_in, chunk).start()
        load(1, values, v_in, chunk).start()
        load(2, query, scaled, chunks - 1 - chunk).start()
        load(3, grad, g_in, chunks - 1 - chunk).start()

    barrier = pltpu.get_barrier_semaphore()

    @pl.loop(1, n_inner)
    def _(step):
        peer = lax.rem(inner + step, n_inner)
        pl.semaphore_signal(barrier, inc=1, device_id=(outer, peer), device_id_type=MESH)

    @pl.loop(1, n_outer)
    def _(step):
        peer = lax.rem(outer + step, n_outer)
        pl.semaphore_signal(barrier, inc=1, device_id=(peer, inner), device_id_type=MESH)

    first = (outer * n_inner + inner) * rows

    def accumulate(chunk, sums):
        kv, qg = list(sums[:H]), list(sums[H:])
        load(0, keys, k_in, chunk).wait()
        load(1, values, v_in, chunk).wait()
        for b in range(per_chunk):
            block = chunk * per_chunk + b
            span = pl.ds(pl.multiple_of(block * TILE, TILE), TILE)
            for h in range(H):
                cols = slice(h * E, (h + 1) * E)
                kv_local[block, h] = kv[h].astype(BF16)
                kv[h] = kv[h] + dot(k_in[span, cols], v_in[span, cols], TN)
        back = chunks - 1 - chunk
        load(2, query, scaled, back).wait()
        load(3, grad, g_in, back).wait()
        for b in range(per_chunk - 1, -1, -1):
            block = back * per_chunk + b
            span = pl.ds(pl.multiple_of(block * TILE, TILE), TILE)
            scale = coefficient(first + block * TILE, TILE)
            for h in range(H):
                cols = slice(h * E, (h + 1) * E)
                qg_local[block, h] = qg[h].astype(BF16)
                qs = (scaled[span, cols].astype(F32) * scale).astype(BF16)
                scaled[span, cols] = qs
                qg[h] = qg[h] + dot(qs, g_in[span, cols], TN)
        return tuple(kv) + tuple(qg)

    zero = jnp.zeros((E, E), F32)
    sums = lax.fori_loop(0, chunks, accumulate, (zero,) * (2 * H))
    share = n_inner // H
    for h in range(H):
        mine[h * share:(h + 1) * share, 0:part] = sums[h].reshape(share, part, E)
        mine[h * share:(h + 1) * share, part:2 * part] = sums[H + h].reshape(share, part, E)

    row = lax.broadcasted_iota(jnp.int32, (TILE, TILE), 0)
    col = lax.broadcasted_iota(jnp.int32, (TILE, TILE), 1)
    causal = row >= col

    def local_terms(start, stop):
        @pl.loop(start, stop)
        def _(pair):
            for b in range(2):
                block = pair * 2 + b
                span = pl.ds(pl.multiple_of(block * TILE, TILE), TILE)
                qs, k, v, g = scaled[span], k_in[span], v_in[span], g_in[span]
                kv = both_heads(kv_local[block, 0], kv_local[block, 1])
                qg = both_heads(qg_local[block, 0], qg_local[block, 1])
                state_parts = (dot(qs, kv, NN), dot(g, kv, NT), dot(v, qg, NT), dot(k, qg, NN))
                for h in range(H):
                    cols = slice(h * E, (h + 1) * E)
                    a = jnp.where(causal, dot(qs[:, cols], k[:, cols], NT), 0.0).astype(BF16)
                    d = jnp.where(causal, dot(g[:, cols], v[:, cols], NT), 0.0).astype(BF16)
                    att_sum[span, cols] = dot(a, v[:, cols], NN) + state_parts[0][:, cols]
                    qgrad_sum[span, cols] = dot(d, k[:, cols], NN) + state_parts[1][:, cols]
                    kgrad_sum[span, cols] = dot(d, qs[:, cols], TN) + state_parts[2][:, cols]
                    vgrad_sum[span, cols] = dot(a, g[:, cols], TN) + state_parts[3][:, cols]

    pl.semaphore_wait(barrier, n_inner + n_outer - 2)

    def over_inner(source, target, send, recv, step, slot):
        peer = lax.rem(inner + step, n_inner)
        slot = inner if slot is None else peer
        return pltpu.make_async_remote_copy(
            src_ref=source.at[peer], dst_ref=target.at[slot],
            send_sem=send.at[peer], recv_sem=recv.at[slot],
            device_id=(outer, peer), device_id_type=MESH)

    def over_outer(step, slot):
        peer = lax.rem(outer + step, n_outer)
        slot = outer if slot is None else peer
        return pltpu.make_async_remote_copy(
            src_ref=total, dst_ref=totals.at[slot],
            send_sem=send_b.at[peer], recv_sem=recv_b.at[slot],
            device_id=(peer, inner), device_id_type=MESH)

    @pl.loop(1, n_inner)
    def _(step):
        over_inner(mine, arrived, send_a, recv_a, step, None).start()

    arrived[inner] = mine[inner]
    local_terms(0, SPLIT[0])

    @pl.loop(1, n_inner)
    def _(step):
        over_inner(mine, arrived, send_a, recv_a, step, 1).wait_recv()

    kv = jnp.zeros((part, E), F32)
    qg = jnp.zeros((part, E), F32)
    for j in range(n_inner):
        done[j, 0:part] = kv
        kv = kv + arrived[j, 0:part]
        k = n_inner - 1 - j
        done[k, part:2 * part] = qg
        qg = qg + arrived[k, part:2 * part]
    total[0:part] = kv
    total[part:2 * part] = qg

    @pl.loop(1, n_outer)
    def _(step):
        over_outer(step, None).start()

    totals[outer] = total[...]
    local_terms(SPLIT[0], SPLIT[1])

    @pl.loop(1, n_outer)
    def _(step):
        over_outer(step, 1).wait_recv()

    kv = jnp.zeros((part, E), F32)
    qg = jnp.zeros((part, E), F32)
    for j in range(n_outer):
        kv = kv + jnp.where(j < outer, totals[j, 0:part], 0.0)
        qg = qg + jnp.where(j > outer, totals[j, part:2 * part], 0.0)
    for j in range(n_inner):
        done[j, 0:part] = done[j, 0:part] + kv
        done[j, part:2 * part] = done[j, part:2 * part] + qg

    @pl.loop(1, n_inner)
    def _(step):
        over_inner(done, finished, send_c, recv_c, step, None).start()

    finished[inner] = done[inner]
    local_terms(SPLIT[1], SPLIT[2])

    @pl.loop(1, n_inner)
    def _(step):
        over_inner(done, finished, send_c, recv_c, step, 1).wait_recv()

    for h in range(H):
        span = slice(h * share, (h + 1) * share)
        before[0, h] = finished[span, 0:part].reshape(E, E).astype(BF16)
        before[1, h] = finished[span, part:2 * part].reshape(E, E).astype(BF16)

    @pl.loop(1, n_inner)
    def _(step):
        over_inner(mine, arrived, send_a, recv_a, step, None).wait_send()
        over_inner(done, finished, send_c, recv_c, step, None).wait_send()

    @pl.loop(1, n_outer)
    def _(step):
        over_outer(step, None).wait_send()


def finish_kernel(
    n_inner, scaled, k_in, v_in, g_in, att_sum, qgrad_sum, kgrad_sum, vgrad_sum, before,
    attended, qgrad, kgrad, vgrad, att_out, qgrad_out, kgrad_out, vgrad_out, sem,
):
    rows = scaled.shape[0]
    first = (lax.axis_index("outer") * n_inner + lax.axis_index("inner")) * rows
    kv = both_heads(before[0, 0], before[0, 1])
    qg = both_heads(before[1, 0], before[1, 1])

    def store(which, source, target, tile):
        span = pl.ds(pl.multiple_of(tile * OUT, OUT), OUT)
        return pltpu.make_async_copy(source.at[span], target.at[span], sem.at[which, tile])

    stores = ((att_out, attended), (qgrad_out, qgrad), (kgrad_out, kgrad), (vgrad_out, vgrad))

    @pl.loop(0, rows // OUT)
    def _(tile):
        span = pl.ds(pl.multiple_of(tile * OUT, OUT), OUT)
        scale = coefficient(first + tile * OUT, OUT)
        wide = jnp.concatenate([scale] * H, axis=1)
        att_out[span] = (att_sum[span] + dot(scaled[span], kv, NN)).astype(BF16)
        qgrad_out[span] = ((qgrad_sum[span] + dot(g_in[span], kv, NT)) * wide).astype(BF16)
        kgrad_out[span] = (kgrad_sum[span] + dot(v_in[span], qg, NT)).astype(BF16)
        vgrad_out[span] = (vgrad_sum[span] + dot(k_in[span], qg, NN)).astype(BF16)
        for which, (source, target) in enumerate(stores):
            store(which, source, target, tile).start()

    @pl.loop(0, rows // OUT)
    def _(tile):
        for which, (source, target) in enumerate(stores):
            store(which, source, target, tile).wait()


def on_device(n_outer, n_inner, query, keys, values, out_grad):
    rows, width = query.shape
    blocks = rows // TILE
    part = E * H // n_inner
    anywhere = pl.BlockSpec(memory_space=pl.ANY)
    in_vmem = pl.BlockSpec(memory_space=pltpu.VMEM)
    slices = pltpu.VMEM((n_inner, 2 * part, E), F32)
    dma = pltpu.SemaphoreType.DMA
    data = jax.ShapeDtypeStruct((rows, width), BF16)
    sums = jax.ShapeDtypeStruct((rows, width), F32)
    local = pl.pallas_call(
        functools.partial(local_kernel, n_outer, n_inner),
        out_shape=(data,) * 4 + (sums,) * 4 + (jax.ShapeDtypeStruct((2, H, E, E), BF16),),
        in_specs=[anywhere] * 4,
        out_specs=(in_vmem,) * 9,
        scratch_shapes=[pltpu.VMEM((blocks, H, E, E), BF16)] * 2
        + [slices, slices, slices, pltpu.VMEM((2 * part, E), F32),
           pltpu.VMEM((n_outer, 2 * part, E), F32), slices]
        + [dma((4, rows // CHUNK)), dma((n_inner,)), dma((n_inner,)), dma((n_outer,)),
           dma((n_outer,)), dma((n_inner,)), dma((n_inner,))],
        compiler_params=pltpu.CompilerParams(
            collective_id=0, has_side_effects=True, vmem_limit_bytes=12 << 20),
        name="local",
    )(*[pltpu.with_memory_space_constraint(x, pltpu.HBM) for x in (query, keys, values, out_grad)])
    return pl.pallas_call(
        functools.partial(finish_kernel, n_inner),
        out_shape=(data,) * 4,
        in_specs=[in_vmem] * 9,
        out_specs=(anywhere,) * 4,
        scratch_shapes=[pltpu.VMEM((rows, width), BF16)] * 4 + [dma((4, rows // OUT))],
        compiler_params=pltpu.CompilerParams(vmem_limit_bytes=16 << 20),
        name="finish",
    )(*local)


def solution(mesh):
    spec = P(("outer", "inner"), None)
    return jax.shard_map(
        functools.partial(on_device, mesh.shape["outer"], mesh.shape["inner"]),
        mesh=mesh,
        in_specs=(spec,) * 4,
        out_specs=(spec,) * 4,
        check_vma=False,
    )
```

time: 50.7 us -> 33.9 us (0.67)
  Pallas kernels: 43.5 us -> 33.2 us
  local copies, waits for them, and re-layouts: 6.36 us -> 0 us
    pallas_call x2, Pallas kernels: 43.5 us -> 33.2 us  [the longest x1 28.5 us: on_device(): pl.pallas_call(functools.partial(local_kernel, n_outer, n_inner), out_sha...]
    unnamed x8 -> x0, local copies, waits for them, and re-layouts: 6.36 us -> none
where the time goes in v2:
time: 33.9 us; the launch traced here: 33.8 us
  Pallas kernels  33.2 us (98%)
  between operations  0.64 us (2%)
    pallas_call x1, Pallas kernels, on_device(): pl.pallas_call(functools.partial(local_kernel, n_outer, n_inner), out_sha...  28.5 us
    pallas_call x1, Pallas kernels, on_device(): pl.pallas_call(functools.partial(finish_kernel, n_inner), out_shape=(data...  4.71 us

profile of v2, /device:TPU:0, one launch (start us, length us, event | category | flops | bytes accessed | tf_op | source)
XLA Modules:
  0.0 33.8 jit_solution(8627805999944725003)
XLA Ops:
  0.6 28.5 %local.1 = (bf16[4096,256]{1,0:T(8,128)(2,1)S(1)}, bf16[4096,256]{1,0:T(8,128)(2,1)S(1)}, bf16[4096,256]{1,0:T(8,128)(2,1)S(1)}, bf16[4096,256]{1,0:T(8,128)(2,1...) custom-call(bf16[4096,256]{1,0:T(8,128)(2,1)} %query.1, ...), custom_call_target="tpu_custom_call" | custom-call | tf_op jit(solution)/shard_map/local/pallas_call | solution.py:264
  29.1 4.7 %finish.1 = (bf16[4096,256]{1,0:T(8,128)(2,1)}, bf16[4096,256]{1,0:T(8,128)(2,1)}, bf16[4096,256]{1,0:T(8,128)(2,1)}, bf16[4096,256]{1,0:T(8,128)(2,1)}) custom-call(bf16[4096,256]{1,0:T(8,128)(2,1)S(1)} %get-tuple-element.13.scaled, bf16[4096,256]{1,0:T(8,128)(2,1)S(1)} %get-tuple-element.14.k_in, bf16[4096,256]{1,0:T(8,128)(2,1)S(1)} %get-tuple-element.15.v_in, ...), custom_call_target="tpu_custom_call" | custom-call | tf_op jit(solution)/shard_map/finish/pallas_call | solution.py:278

commit v3 on v2

--- a/solution.py
+++ b/solution.py
@@ -10,9 +10,10 @@
 H = 2
 E = 128
 TILE = 256
-CHUNK = 512
-OUT = 512
-SPLIT = (3, 6, 8)
+CHUNK = 2048
+OUT = 1024
+GROUP = 4
+SPLIT = (2, 3, 4)
 MESH = pl.DeviceIdType.MESH
 F32 = jnp.float32
 BF16 = jnp.bfloat16
@@ -41,7 +42,7 @@
     n_outer, n_inner,
     query, keys, values, grad,
     scaled, k_in, v_in, g_in, att_sum, qgrad_sum, kgrad_sum, vgrad_sum, before,
-    kv_local, qg_local, mine, arrived, done, total, totals, finished,
+    kv_local, qg_local, totals_of, mine, arrived, done, total, totals, finished,
     in_sem, send_a, recv_a, send_b, recv_b, send_c, recv_c,
 ):
     outer = lax.axis_index("outer")
@@ -55,12 +56,12 @@
         span = pl.ds(pl.multiple_of(chunk * CHUNK, CHUNK), CHUNK)
         return pltpu.make_async_copy(source.at[span], target.at[span], in_sem.at[which, chunk])
 
-    @pl.loop(0, chunks)
-    def _(chunk):
+    for chunk in range(chunks):
         load(0, keys, k_in, chunk).start()
         load(1, values, v_in, chunk).start()
-        load(2, query, scaled, chunks - 1 - chunk).start()
-        load(3, grad, g_in, chunks - 1 - chunk).start()
+    for chunk in reversed(range(chunks)):
+        load(2, query, scaled, chunk).start()
+        load(3, grad, g_in, chunk).start()
 
     barrier = pltpu.get_barrier_semaphore()
 
@@ -76,38 +77,44 @@
 
     first = (outer * n_inner + inner) * rows
 
-    def accumulate(chunk, sums):
-        kv, qg = list(sums[:H]), list(sums[H:])
+    totals_of[...] = jnp.zeros_like(totals_of)
+
+    @pl.loop(0, chunks)
+    def _(chunk):
         load(0, keys, k_in, chunk).wait()
         load(1, values, v_in, chunk).wait()
-        for b in range(per_chunk):
-            block = chunk * per_chunk + b
-            span = pl.ds(pl.multiple_of(block * TILE, TILE), TILE)
-            for h in range(H):
-                cols = slice(h * E, (h + 1) * E)
-                kv_local[block, h] = kv[h].astype(BF16)
-                kv[h] = kv[h] + dot(k_in[span, cols], v_in[span, cols], TN)
-        back = chunks - 1 - chunk
-        load(2, query, scaled, back).wait()
-        load(3, grad, g_in, back).wait()
-        for b in range(per_chunk - 1, -1, -1):
-            block = back * per_chunk + b
-            span = pl.ds(pl.multiple_of(block * TILE, TILE), TILE)
-            scale = coefficient(first + block * TILE, TILE)
-            for h in range(H):
-                cols = slice(h * E, (h + 1) * E)
-                qg_local[block, h] = qg[h].astype(BF16)
+        for h in range(H):
+            cols = slice(h * E, (h + 1) * E)
+            kv = totals_of[0, h]
+            for b in range(per_chunk):
+                block = chunk * per_chunk + b
+                span = pl.ds(pl.multiple_of(block * TILE, TILE), TILE)
+                kv_local[block, h] = kv.astype(BF16)
+                kv = kv + dot(k_in[span, cols], v_in[span, cols], TN)
+            totals_of[0, h] = kv
+
+    @pl.loop(0, chunks)
+    def _(turn):
+        chunk = chunks - 1 - turn
+        load(2, query, scaled, chunk).wait()
+        load(3, grad, g_in, chunk).wait()
+        for h in range(H):
+            cols = slice(h * E, (h + 1) * E)
+            qg = totals_of[1, h]
+            for b in reversed(range(per_chunk)):
+                block = chunk * per_chunk + b
+                span = pl.ds(pl.multiple_of(block * TILE, TILE), TILE)
+                scale = coefficient(first + block * TILE, TILE)
+                qg_local[block, h] = qg.astype(BF16)
                 qs = (scaled[span, cols].astype(F32) * scale).astype(BF16)
                 scaled[span, cols] = qs
-                qg[h] = qg[h] + dot(qs, g_in[span, cols], TN)
-        return tuple(kv) + tuple(qg)
-
-    zero = jnp.zeros((E, E), F32)
-    sums = lax.fori_loop(0, chunks, accumulate, (zero,) * (2 * H))
+                qg = qg + dot(qs, g_in[span, cols], TN)
+            totals_of[1, h] = qg
+
     share = n_inner // H
     for h in range(H):
-        mine[h * share:(h + 1) * share, 0:part] = sums[h].reshape(share, part, E)
-        mine[h * share:(h + 1) * share, part:2 * part] = sums[H + h].reshape(share, part, E)
+        for s in range(2):
+            mine[h * share:(h + 1) * share, s * part:(s + 1) * part] = totals_of[s, h].reshape(share, part, E)
 
     row = lax.broadcasted_iota(jnp.int32, (TILE, TILE), 0)
     col = lax.broadcasted_iota(jnp.int32, (TILE, TILE), 1)
@@ -115,51 +122,60 @@
 
     def local_terms(start, stop):
         @pl.loop(start, stop)
-        def _(pair):
-            for b in range(2):
-                block = pair * 2 + b
+        def _(group):
+            for b in range(GROUP):
+                block = group * GROUP + b
                 span = pl.ds(pl.multiple_of(block * TILE, TILE), TILE)
-                qs, k, v, g = scaled[span], k_in[span], v_in[span], g_in[span]
-                kv = both_heads(kv_local[block, 0], kv_local[block, 1])
-                qg = both_heads(qg_local[block, 0], qg_local[block, 1])
-                state_parts = (dot(qs, kv, NN), dot(g, kv, NT), dot(v, qg, NT), dot(k, qg, NN))
                 for h in range(H):
                     cols = slice(h * E, (h + 1) * E)
-                    a = jnp.where(causal, dot(qs[:, cols], k[:, cols], NT), 0.0).astype(BF16)
-                    d = jnp.where(causal, dot(g[:, cols], v[:, cols], NT), 0.0).astype(BF16)
-                    att_sum[span, cols] = dot(a, v[:, cols], NN) + state_parts[0][:, cols]
-                    qgrad_sum[span, cols] = dot(d, k[:, cols], NN) + state_parts[1][:, cols]
-                    kgrad_sum[span, cols] = dot(d, qs[:, cols], TN) + state_parts[2][:, cols]
-                    vgrad_sum[span, cols] = dot(a, g[:, cols], TN) + state_parts[3][:, cols]
+                    qs, k, v, g = scaled[span, cols], k_in[span, cols], v_in[span, cols], g_in[span, cols]
+                    kv, qg = kv_local[block, h], qg_local[block, h]
+                    a = jnp.where(causal, dot(qs, k, NT), 0.0).astype(BF16)
+                    d = jnp.where(causal, dot(g, v, NT), 0.0).astype(BF16)
+                    att_sum[span, cols] = dot(
+                        jnp.concatenate([a, qs], axis=1), jnp.concatenate([v, kv], axis=0), NN)
+                    qgrad_sum[span, cols] = dot(
+                        jnp.concatenate([d, g], axis=1), jnp.concatenate([k, kv.T], axis=0), NN)
+                    kgrad_sum[span, cols] = dot(d, qs, TN) + dot(v, qg, NT)
+                    vgrad_sum[span, cols] = dot(a, g, TN) + dot(k, qg, NN)
 
     pl.semaphore_wait(barrier, n_inner + n_outer - 2)
 
-    def over_inner(source, target, send, recv, step, slot):
-        peer = lax.rem(inner + step, n_inner)
-        slot = inner if slot is None else peer
+    side = 4
+    plane = [(a, b) for a in range(n_inner // side) for b in range(side) if (a, b) != (0, 0)]
+    plane.sort(key=lambda o: -min(o[0], n_inner // side - o[0]) - min(o[1], side - o[1]))
+    line = [(a, b) for a in range(n_outer // 2) for b in range(2) if (a, b) != (0, 0)]
+    line.sort(key=lambda o: -3 * min(o[0], n_outer // 2 - o[0]) - o[1])
+
+    def shifted(place, offset, width, sizes, sign):
+        high = lax.rem(place // width + sizes + sign * offset[0], sizes)
+        low = lax.rem(lax.rem(place, width) + width + sign * offset[1], width)
+        return high * width + low
+
+    def over_inner(source, target, send, recv, offset, landing=False):
+        peer = shifted(inner, offset, side, n_inner // side, 1)
+        slot = shifted(inner, offset, side, n_inner // side, -1) if landing else inner
         return pltpu.make_async_remote_copy(
             src_ref=source.at[peer], dst_ref=target.at[slot],
             send_sem=send.at[peer], recv_sem=recv.at[slot],
             device_id=(outer, peer), device_id_type=MESH)
 
-    def over_outer(step, slot):
-        peer = lax.rem(outer + step, n_outer)
-        slot = outer if slot is None else peer
+    def over_outer(offset, landing=False):
+        peer = shifted(outer, offset, 2, n_outer // 2, 1)
+        slot = shifted(outer, offset, 2, n_outer // 2, -1) if landing else outer
         return pltpu.make_async_remote_copy(
             src_ref=total, dst_ref=totals.at[slot],
             send_sem=send_b.at[peer], recv_sem=recv_b.at[slot],
             device_id=(peer, inner), device_id_type=MESH)
 
-    @pl.loop(1, n_inner)
-    def _(step):
-        over_inner(mine, arrived, send_a, recv_a, step, None).start()
+    for offset in plane:
+        over_inner(mine, arrived, send_a, recv_a, offset).start()
 
     arrived[inner] = mine[inner]
     local_terms(0, SPLIT[0])
 
-    @pl.loop(1, n_inner)
-    def _(step):
-        over_inner(mine, arrived, send_a, recv_a, step, 1).wait_recv()
+    for offset in reversed(plane):
+        over_inner(mine, arrived, send_a, recv_a, offset, True).wait_recv()
 
     kv = jnp.zeros((part, E), F32)
     qg = jnp.zeros((part, E), F32)
@@ -172,16 +188,14 @@
     total[0:part] = kv
     total[part:2 * part] = qg
 
-    @pl.loop(1, n_outer)
-    def _(step):
-        over_outer(step, None).start()
+    for offset in line:
+        over_outer(offset).start()
 
     totals[outer] = total[...]
     local_terms(SPLIT[0], SPLIT[1])
 
-    @pl.loop(1, n_outer)
-    def _(step):
-        over_outer(step, 1).wait_recv()
+    for offset in reversed(line):
+        over_outer(offset, True).wait_recv()
 
     kv = jnp.zeros((part, E), F32)
     qg = jnp.zeros((part, E), F32)
@@ -192,30 +206,25 @@
         done[j, 0:part] = done[j, 0:part] + kv
         done[j, part:2 * part] = done[j, part:2 * part] + qg
 
-    @pl.loop(1, n_inner)
-    def _(step):
-        over_inner(done, finished, send_c, recv_c, step, None).start()
+    for offset in plane:
+        over_inner(done, finished, send_c, recv_c, offset).start()
 
     finished[inner] = done[inner]
     local_terms(SPLIT[1], SPLIT[2])
 
-    @pl.loop(1, n_inner)
-    def _(step):
-        over_inner(done, finished, send_c, recv_c, step, 1).wait_recv()
+    for offset in reversed(plane):
+        over_inner(done, finished, send_c, recv_c, offset, True).wait_recv()
 
     for h in range(H):
         span = slice(h * share, (h + 1) * share)
         before[0, h] = finished[span, 0:part].reshape(E, E).astype(BF16)
         before[1, h] = finished[span, part:2 * part].reshape(E, E).astype(BF16)
 
-    @pl.loop(1, n_inner)
-    def _(step):
-        over_inner(mine, arrived, send_a, recv_a, step, None).wait_send()
-        over_inner(done, finished, send_c, recv_c, step, None).wait_send()
-
-    @pl.loop(1, n_outer)
-    def _(step):
-        over_outer(step, None).wait_send()
+    for offset in plane:
+        over_inner(mine, arrived, send_a, recv_a, offset).wait_send()
+        over_inner(done, finished, send_c, recv_c, offset).wait_send()
+    for offset in line:
+        over_outer(offset).wait_send()
 
 
 def finish_kernel(
@@ -267,7 +276,7 @@
         in_specs=[anywhere] * 4,
         out_specs=(in_vmem,) * 9,
         scratch_shapes=[pltpu.VMEM((blocks, H, E, E), BF16)] * 2
-        + [slices, slices, slices, pltpu.VMEM((2 * part, E), F32),
+        + [pltpu.VMEM((2, H, E, E), F32), slices, slices, slices, pltpu.VMEM((2 * part, E), F32),
            pltpu.VMEM((n_outer, 2 * part, E), F32), slices]
         + [dma((4, rows // CHUNK)), dma((n_inner,)), dma((n_inner,)), dma((n_outer,)),
            dma((n_outer,)), dma((n_inner,)), dma((n_inner,))],

time: 33.9 us -> 30.1 us (0.89)
  Pallas kernels: 33.2 us -> 29.3 us
    pallas_call x1, Pallas kernels: 28.5 us -> 25.2 us  [on_device(): pl.pallas_call(functools.partial(local_kernel, n_outer, n_inner), out_sha...]
    pallas_call x1, Pallas kernels: 4.71 us -> 4.18 us  [on_device(): pl.pallas_call(functools.partial(finish_kernel, n_inner), out_shape=(data...]
where the time goes in v3:
time: 30.1 us; the launch traced here: 30 us
  Pallas kernels  29.3 us (97%)
  between operations  0.64 us (2%)
    pallas_call x1, Pallas kernels, on_device(): pl.pallas_call(functools.partial(local_kernel, n_outer, n_inner), out_sha...  25.2 us
    pallas_call x1, Pallas kernels, on_device(): pl.pallas_call(functools.partial(finish_kernel, n_inner), out_shape=(data...  4.18 us

profile of v3, /device:TPU:0, one launch (start us, length us, event | category | flops | bytes accessed | tf_op | source)
XLA Modules:
  0.0 30.0 jit_solution(11127821048241323920)
XLA Ops:
  0.6 25.2 %local.1 = (bf16[4096,256]{1,0:T(8,128)(2,1)S(1)}, bf16[4096,256]{1,0:T(8,128)(2,1)S(1)}, bf16[4096,256]{1,0:T(8,128)(2,1)S(1)}, bf16[4096,256]{1,0:T(8,128)(2,1...) custom-call(bf16[4096,256]{1,0:T(8,128)(2,1)} %query.1, ...), custom_call_target="tpu_custom_call" | custom-call | tf_op jit(solution)/shard_map/local/pallas_call | solution.py:273
  25.8 4.2 %finish.1 = (bf16[4096,256]{1,0:T(8,128)(2,1)}, bf16[4096,256]{1,0:T(8,128)(2,1)}, bf16[4096,256]{1,0:T(8,128)(2,1)}, bf16[4096,256]{1,0:T(8,128)(2,1)}) custom-call(bf16[4096,256]{1,0:T(8,128)(2,1)S(1)} %get-tuple-element.13.scaled, bf16[4096,256]{1,0:T(8,128)(2,1)S(1)} %get-tuple-element.14.k_in, bf16[4096,256]{1,0:T(8,128)(2,1)S(1)} %get-tuple-element.15.v_in, ...), custom_call_target="tpu_custom_call" | custom-call | tf_op jit(solution)/shard_map/finish/pallas_call | solution.py:287

commit v4 on v3

--- a/solution.py
+++ b/solution.py
@@ -11,9 +11,8 @@
 E = 128
 TILE = 256
 CHUNK = 2048
-OUT = 1024
-GROUP = 4
-SPLIT = (2, 3, 4)
+SIZES = (512,) * 8
+SPLIT = (6, 12, 16)
 MESH = pl.DeviceIdType.MESH
 F32 = jnp.float32
 BF16 = jnp.bfloat16
@@ -63,6 +62,7 @@
         load(2, query, scaled, chunk).start()
         load(3, grad, g_in, chunk).start()
 
+    totals[...] = jnp.zeros_like(totals)
     barrier = pltpu.get_barrier_semaphore()
 
     @pl.loop(1, n_inner)
@@ -121,23 +121,20 @@
     causal = row >= col
 
     def local_terms(start, stop):
-        @pl.loop(start, stop)
-        def _(group):
-            for b in range(GROUP):
-                block = group * GROUP + b
-                span = pl.ds(pl.multiple_of(block * TILE, TILE), TILE)
-                for h in range(H):
-                    cols = slice(h * E, (h + 1) * E)
-                    qs, k, v, g = scaled[span, cols], k_in[span, cols], v_in[span, cols], g_in[span, cols]
-                    kv, qg = kv_local[block, h], qg_local[block, h]
-                    a = jnp.where(causal, dot(qs, k, NT), 0.0).astype(BF16)
-                    d = jnp.where(causal, dot(g, v, NT), 0.0).astype(BF16)
-                    att_sum[span, cols] = dot(
-                        jnp.concatenate([a, qs], axis=1), jnp.concatenate([v, kv], axis=0), NN)
-                    qgrad_sum[span, cols] = dot(
-                        jnp.concatenate([d, g], axis=1), jnp.concatenate([k, kv.T], axis=0), NN)
-                    kgrad_sum[span, cols] = dot(d, qs, TN) + dot(v, qg, NT)
-                    vgrad_sum[span, cols] = dot(a, g, TN) + dot(k, qg, NN)
+        for block in range(start, stop):
+            span = pl.ds(block * TILE, TILE)
+            for h in range(H):
+                cols = slice(h * E, (h + 1) * E)
+                qs, k, v, g = scaled[span, cols], k_in[span, cols], v_in[span, cols], g_in[span, cols]
+                kv, qg = kv_local[block, h], qg_local[block, h]
+                a = jnp.where(causal, dot(qs, k, NT), 0.0).astype(BF16)
+                d = jnp.where(causal, dot(g, v, NT), 0.0).astype(BF16)
+                att_sum[span, cols] = dot(
+                    jnp.concatenate([a, qs], axis=1), jnp.concatenate([v, kv], axis=0), NN)
+                qgrad_sum[span, cols] = dot(
+                    jnp.concatenate([d, g], axis=1), jnp.concatenate([k, kv.T], axis=0), NN)
+                kgrad_sum[span, cols] = dot(d, qs, TN) + dot(v, qg, NT)
+                vgrad_sum[span, cols] = dot(a, g, TN) + dot(k, qg, NN)
 
     pl.semaphore_wait(barrier, n_inner + n_outer - 2)
 
@@ -163,8 +160,11 @@
     def over_outer(offset, landing=False):
         peer = shifted(outer, offset, 2, n_outer // 2, 1)
         slot = shifted(outer, offset, 2, n_outer // 2, -1) if landing else outer
+        goal = outer if landing else peer
+        half = 1 - (goal + n_outer - slot) // n_outer
+        span = pl.ds(pl.multiple_of(half * part, part), part)
         return pltpu.make_async_remote_copy(
-            src_ref=total, dst_ref=totals.at[slot],
+            src_ref=total.at[span], dst_ref=totals.at[slot, span],
             send_sem=send_b.at[peer], recv_sem=recv_b.at[slot],
             device_id=(peer, inner), device_id_type=MESH)
 
@@ -176,6 +176,17 @@
 
     for offset in reversed(plane):
         over_inner(mine, arrived, send_a, recv_a, offset, True).wait_recv()
+
+    kv = arrived[0, 0:part]
+    qg = arrived[0, part:2 * part]
+    for j in range(1, n_inner):
+        kv = kv + arrived[j, 0:part]
+        qg = qg + arrived[j, part:2 * part]
+    total[0:part] = kv
+    total[part:2 * part] = qg
+
+    for offset in line:
+        over_outer(offset).start()
 
     kv = jnp.zeros((part, E), F32)
     qg = jnp.zeros((part, E), F32)
@@ -185,13 +196,7 @@
         k = n_inner - 1 - j
         done[k, part:2 * part] = qg
         qg = qg + arrived[k, part:2 * part]
-    total[0:part] = kv
-    total[part:2 * part] = qg
-
-    for offset in line:
-        over_outer(offset).start()
-
-    totals[outer] = total[...]
+
     local_terms(SPLIT[0], SPLIT[1])
 
     for offset in reversed(line):
@@ -200,8 +205,8 @@
     kv = jnp.zeros((part, E), F32)
     qg = jnp.zeros((part, E), F32)
     for j in range(n_outer):
-        kv = kv + jnp.where(j < outer, totals[j, 0:part], 0.0)
-        qg = qg + jnp.where(j > outer, totals[j, part:2 * part], 0.0)
+        kv = kv + totals[j, 0:part]
+        qg = qg + totals[j, part:2 * part]
     for j in range(n_inner):
         done[j, 0:part] = done[j, 0:part] + kv
         done[j, part:2 * part] = done[j, part:2 * part] + qg
@@ -236,28 +241,31 @@
     kv = both_heads(before[0, 0], before[0, 1])
     qg = both_heads(before[1, 0], before[1, 1])
 
+    tiles = []
+    start = 0
+    for size in SIZES:
+        tiles.append((start, size))
+        start += size
+
     def store(which, source, target, tile):
-        span = pl.ds(pl.multiple_of(tile * OUT, OUT), OUT)
+        span = pl.ds(*tiles[tile])
         return pltpu.make_async_copy(source.at[span], target.at[span], sem.at[which, tile])
 
     stores = ((att_out, attended), (qgrad_out, qgrad), (kgrad_out, kgrad), (vgrad_out, vgrad))
-
-    @pl.loop(0, rows // OUT)
-    def _(tile):
-        span = pl.ds(pl.multiple_of(tile * OUT, OUT), OUT)
-        scale = coefficient(first + tile * OUT, OUT)
-        wide = jnp.concatenate([scale] * H, axis=1)
+    for tile, (start, size) in enumerate(tiles):
+        span = pl.ds(start, size)
         att_out[span] = (att_sum[span] + dot(scaled[span], kv, NN)).astype(BF16)
+        store(0, *stores[0], tile).start()
+        kgrad_out[span] = (kgrad_sum[span] + dot(v_in[span], qg, NT)).astype(BF16)
+        store(2, *stores[2], tile).start()
+        vgrad_out[span] = (vgrad_sum[span] + dot(k_in[span], qg, NN)).astype(BF16)
+        store(3, *stores[3], tile).start()
+        wide = jnp.concatenate([coefficient(first + start, size)] * H, axis=1)
         qgrad_out[span] = ((qgrad_sum[span] + dot(g_in[span], kv, NT)) * wide).astype(BF16)
-        kgrad_out[span] = (kgrad_sum[span] + dot(v_in[span], qg, NT)).astype(BF16)
-        vgrad_out[span] = (vgrad_sum[span] + dot(k_in[span], qg, NN)).astype(BF16)
-        for which, (source, target) in enumerate(stores):
-            store(which, source, target, tile).start()
-
-    @pl.loop(0, rows // OUT)
-    def _(tile):
-        for which, (source, target) in enumerate(stores):
-            store(which, source, target, tile).wait()
+        store(1, *stores[1], tile).start()
+    for tile in range(len(tiles)):
+        for which, pair in enumerate(stores):
+            store(which, *pair, tile).wait()
 
 
 def on_device(n_outer, n_inner, query, keys, values, out_grad):
@@ -289,7 +297,7 @@
         out_shape=(data,) * 4,
         in_specs=[in_vmem] * 9,
         out_specs=(anywhere,) * 4,
-        scratch_shapes=[pltpu.VMEM((rows, width), BF16)] * 4 + [dma((4, rows // OUT))],
+        scratch_shapes=[pltpu.VMEM((rows, width), BF16)] * 4 + [dma((4, len(SIZES)))],
         compiler_params=pltpu.CompilerParams(vmem_limit_bytes=16 << 20),
         name="finish",
     )(*local)

time: 30.1 us -> 29 us (0.963)
  Pallas kernels: 29.3 us -> 28.3 us
    pallas_call x1, Pallas kernels: 25.2 us -> 24.4 us  [on_device(): pl.pallas_call(functools.partial(local_kernel, n_outer, n_inner), out_sha...]
    pallas_call x1, Pallas kernels: 4.18 us -> 3.83 us  [on_device(): pl.pallas_call(functools.partial(finish_kernel, n_inner), out_shape=(data...]
where the time goes in v4:
time: 29 us; the launch traced here: 28.9 us
  Pallas kernels  28.3 us (98%)
  between operations  0.64 us (2%)
    pallas_call x1, Pallas kernels, on_device(): pl.pallas_call(functools.partial(local_kernel, n_outer, n_inner), out_sha...  24.4 us
    pallas_call x1, Pallas kernels, on_device(): pl.pallas_call(functools.partial(finish_kernel, n_inner), out_shape=(data...  3.83 us

profile of v4, /device:TPU:0, one launch (start us, length us, event | category | flops | bytes accessed | tf_op | source)
XLA Modules:
  0.0 28.9 jit_solution(11798113761215746954)
XLA Ops:
  0.6 24.4 %local.1 = (bf16[4096,256]{1,0:T(8,128)(2,1)S(1)}, bf16[4096,256]{1,0:T(8,128)(2,1)S(1)}, bf16[4096,256]{1,0:T(8,128)(2,1)S(1)}, bf16[4096,256]{1,0:T(8,128)(2,1...) custom-call(bf16[4096,256]{1,0:T(8,128)(2,1)} %query.1, ...), custom_call_target="tpu_custom_call" | custom-call | tf_op jit(solution)/shard_map/local/pallas_call | solution.py:281
  25.1 3.8 %finish.1 = (bf16[4096,256]{1,0:T(8,128)(2,1)}, bf16[4096,256]{1,0:T(8,128)(2,1)}, bf16[4096,256]{1,0:T(8,128)(2,1)}, bf16[4096,256]{1,0:T(8,128)(2,1)}) custom-call(bf16[4096,256]{1,0:T(8,128)(2,1)S(1)} %get-tuple-element.13.scaled, bf16[4096,256]{1,0:T(8,128)(2,1)S(1)} %get-tuple-element.14.k_in, bf16[4096,256]{1,0:T(8,128)(2,1)S(1)} %get-tuple-element.15.v_in, ...), custom_call_target="tpu_custom_call" | custom-call | tf_op jit(solution)/shard_map/finish/pallas_call | solution.py:295

commit v5 on v4

--- a/solution.py
+++ b/solution.py
@@ -12,7 +12,7 @@
 TILE = 256
 CHUNK = 2048
 SIZES = (512,) * 8
-SPLIT = (6, 12, 16)
+SPLIT = (7, 13, 16)
 MESH = pl.DeviceIdType.MESH
 F32 = jnp.float32
 BF16 = jnp.bfloat16
@@ -62,17 +62,29 @@
         load(2, query, scaled, chunk).start()
         load(3, grad, g_in, chunk).start()
 
+    side = 4
+    plane = [(a, b) for a in range(n_inner // side) for b in range(side) if (a, b) != (0, 0)]
+    plane.sort(key=lambda o: -min(o[0], n_inner // side - o[0]) - min(o[1], side - o[1]))
+    line = [(a, b) for a in range(n_outer // 2) for b in range(2) if (a, b) != (0, 0)]
+    line.sort(key=lambda o: -3 * min(o[0], n_outer // 2 - o[0]) - o[1])
+
+    def shifted(place, offset, width, sizes):
+        high = lax.rem(place // width + offset[0], sizes)
+        low = lax.rem(lax.rem(place, width) + offset[1], width)
+        return high * width + low
+
+    there = {o: shifted(inner, o, side, n_inner // side) for o in plane}
+    across = {o: shifted(outer, o, 2, n_outer // 2) for o in line}
+
+    def back(offset, high, low):
+        return (high - offset[0]) % high, (low - offset[1]) % low
+
     totals[...] = jnp.zeros_like(totals)
     barrier = pltpu.get_barrier_semaphore()
 
-    @pl.loop(1, n_inner)
-    def _(step):
-        peer = lax.rem(inner + step, n_inner)
+    for peer in there.values():
         pl.semaphore_signal(barrier, inc=1, device_id=(outer, peer), device_id_type=MESH)
-
-    @pl.loop(1, n_outer)
-    def _(step):
-        peer = lax.rem(outer + step, n_outer)
+    for peer in across.values():
         pl.semaphore_signal(barrier, inc=1, device_id=(peer, inner), device_id_type=MESH)
 
     first = (outer * n_inner + inner) * rows
@@ -138,28 +150,17 @@
 
     pl.semaphore_wait(barrier, n_inner + n_outer - 2)
 
-    side = 4
-    plane = [(a, b) for a in range(n_inner // side) for b in range(side) if (a, b) != (0, 0)]
-    plane.sort(key=lambda o: -min(o[0], n_inner // side - o[0]) - min(o[1], side - o[1]))
-    line = [(a, b) for a in range(n_outer // 2) for b in range(2) if (a, b) != (0, 0)]
-    line.sort(key=lambda o: -3 * min(o[0], n_outer // 2 - o[0]) - o[1])
-
-    def shifted(place, offset, width, sizes, sign):
-        high = lax.rem(place // width + sizes + sign * offset[0], sizes)
-        low = lax.rem(lax.rem(place, width) + width + sign * offset[1], width)
-        return high * width + low
-
     def over_inner(source, target, send, recv, offset, landing=False):
-        peer = shifted(inner, offset, side, n_inner // side, 1)
-        slot = shifted(inner, offset, side, n_inner // side, -1) if landing else inner
+        peer = there[offset]
+        slot = there[back(offset, n_inner // side, side)] if landing else inner
         return pltpu.make_async_remote_copy(
             src_ref=source.at[peer], dst_ref=target.at[slot],
             send_sem=send.at[peer], recv_sem=recv.at[slot],
             device_id=(outer, peer), device_id_type=MESH)
 
     def over_outer(offset, landing=False):
-        peer = shifted(outer, offset, 2, n_outer // 2, 1)
-        slot = shifted(outer, offset, 2, n_outer // 2, -1) if landing else outer
+        peer = across[offset]
+        slot = across[back(offset, n_outer // 2, 2)] if landing else outer
         goal = outer if landing else peer
         half = 1 - (goal + n_outer - slot) // n_outer
         span = pl.ds(pl.multiple_of(half * part, part), part)
@@ -216,6 +217,10 @@
 
     finished[inner] = done[inner]
     local_terms(SPLIT[1], SPLIT[2])
+    for offset in plane:
+        over_inner(mine, arrived, send_a, recv_a, offset).wait_send()
+    for offset in line:
+        over_outer(offset).wait_send()
 
     for offset in reversed(plane):
         over_inner(done, finished, send_c, recv_c, offset, True).wait_recv()
@@ -226,10 +231,7 @@
         before[1, h] = finished[span, part:2 * part].reshape(E, E).astype(BF16)
 
     for offset in plane:
-        over_inner(mine, arrived, send_a, recv_a, offset).wait_send()
         over_inner(done, finished, send_c, recv_c, offset).wait_send()
-    for offset in line:
-        over_outer(offset).wait_send()
 
 
 def finish_kernel(

time: 29 us -> 29 us (level)
  no operation moved by 1% of the time
where the time goes in v5:
time: 29 us; the launch traced here: 28.8 us
  Pallas kernels  28.2 us (97%)
  between operations  0.64 us (2%)
    pallas_call x1, Pallas kernels, on_device(): pl.pallas_call(functools.partial(local_kernel, n_outer, n_inner), out_sha...  24.4 us
    pallas_call x1, Pallas kernels, on_device(): pl.pallas_call(functools.partial(finish_kernel, n_inner), out_shape=(data...  3.83 us

profile of v5, /device:TPU:0, one launch (start us, length us, event | category | flops | bytes accessed | tf_op | source)
XLA Modules:
  0.0 28.8 jit_solution(1791235476733114248)
XLA Ops:
  0.6 24.4 %local.1 = (bf16[4096,256]{1,0:T(8,128)(2,1)S(1)}, bf16[4096,256]{1,0:T(8,128)(2,1)S(1)}, bf16[4096,256]{1,0:T(8,128)(2,1)S(1)}, bf16[4096,256]{1,0:T(8,128)(2,1...) custom-call(bf16[4096,256]{1,0:T(8,128)(2,1)} %query.1, ...), custom_call_target="tpu_custom_call" | custom-call | tf_op jit(solution)/shard_map/local/pallas_call | solution.py:283
  25.0 3.8 %finish.1 = (bf16[4096,256]{1,0:T(8,128)(2,1)}, bf16[4096,256]{1,0:T(8,128)(2,1)}, bf16[4096,256]{1,0:T(8,128)(2,1)}, bf16[4096,256]{1,0:T(8,128)(2,1)}) custom-call(bf16[4096,256]{1,0:T(8,128)(2,1)S(1)} %get-tuple-element.13.scaled, bf16[4096,256]{1,0:T(8,128)(2,1)S(1)} %get-tuple-element.14.k_in, bf16[4096,256]{1,0:T(8,128)(2,1)S(1)} %get-tuple-element.15.v_in, ...), custom_call_target="tpu_custom_call" | custom-call | tf_op jit(solution)/shard_map/finish/pallas_call | solution.py:297
